TPU v7x, 32 devices: a whole 2x2x4 slice. The times are simulated.
32 devices in a mesh: seq: 16 (over z, y, core), chan: 2 (over x).
Axes of the slice: x: 2, y: 2, z: 4, core: 2. Of those that a mesh axis runs over, the one named last changes fastest.
Arguments:
- stream_in: bfloat16 [4096, 4096], P('seq'), may hold values from -6 to 6
- mr_proj: bfloat16 [4096, 3, 4096], P('seq', None, 'chan'), may hold values from -6 to 6
- mr_short: float32 [3, 3, 4096], P(None, None, 'chan'), may hold values from -3 to 3
- mr_filter: float32 [256, 128], P('chan'), may hold values from -0.5 to 0.5
- mr_out: bfloat16 [4096, 4096], P('chan', 'seq'), may hold values from -0.09375 to 0.09375
- li_gain: float32 [4096], replicated, may hold values from 0.5 to 1.5
- li_in: bfloat16 [4096, 3, 4096], P('seq', None, 'chan'), may hold values from -0.09375 to 0.09375
- li_short: float32 [3, 3, 4096], P(None, None, 'chan'), may hold values from -3 to 3
- li_res: float32 [16, 4096], P(None, 'chan'), may hold values from -0.09 to 0.09
- li_rate: float32 [16, 4096], P(None, 'chan'), may hold values from 0.00012207031 to 0.05
- li_skip: float32 [4096], P('chan'), may hold values from -4 to 4
Outputs:
- stream_out: bfloat16 [4096, 4096], P('seq', 'chan')
- li_output: bfloat16 [4096, 4096], P('chan', 'seq')
All inputs are finite; a program needn't handle non-finite values.
Results may differ from a plain program's by a relative error of at most 0.04.
Values may be sent and summed in bfloat16 or wider, within the bound.
A program may use at most 128 MiB of HBM per device.

v0:
```python
import jax
import jax.numpy as jnp
from jax import lax
from jax.sharding import PartitionSpec as P

GROUP = 16


EPSILON = 1e-06
HIGHEST = lax.Precision.HIGHEST


def passed_along(block, axis, distance):
    devices = range(lax.axis_size(axis))
    route = [(i - distance, i) for i in devices if i - distance in devices]
    return lax.ppermute(block, axis, route)


def band_matrices(filters):
    tap_count = filters.shape[1]
    out_index = jnp.arange(tap_count, dtype=jnp.int32)[:, None, None]
    in_index = jnp.arange(2 * tap_count, dtype=jnp.int32)[None, :, None]
    lag_index = jnp.arange(tap_count, dtype=jnp.int32)[None, None, :]
    selector = (out_index + tap_count - 1 - in_index == lag_index).astype(jnp.bfloat16)
    high_part = filters.astype(jnp.bfloat16)
    remainder = filters - high_part.astype(jnp.float32)
    middle_part = remainder.astype(jnp.bfloat16)
    low_part = (remainder - middle_part.astype(jnp.float32)).astype(jnp.bfloat16)
    total = jnp.einsum("gj,isj->gis", high_part, selector, preferred_element_type=jnp.float32)
    total = total + jnp.einsum(
        "gj,isj->gis", middle_part, selector, preferred_element_type=jnp.float32
    )
    return total + jnp.einsum("gj,isj->gis", low_part, selector, preferred_element_type=jnp.float32)


def split_product(form, wide_operand, narrow_operand):
    high_part = wide_operand.astype(jnp.bfloat16)
    low_part = (wide_operand - high_part.astype(jnp.float32)).astype(jnp.bfloat16)
    first = jnp.einsum(form, high_part, narrow_operand, preferred_element_type=jnp.float32)
    return first + jnp.einsum(form, low_part, narrow_operand, preferred_element_type=jnp.float32)


def lagged_rows(extended, weights, row_count):
    running = weights[:, 0][None] * extended[2 : 2 + row_count]
    for lag_index in (1, 2):
        running = (
            running
            + weights[:, lag_index][None] * extended[2 - lag_index : 2 - lag_index + row_count]
        )
    return running


def lagged_columns(extended, weights, column_count):
    running = weights[:, 0, :, None] * extended[:, :, 2 : 2 + column_count]
    for lag_index in (1, 2):
        running = (
            running
            + weights[:, lag_index, :, None]
            * extended[:, :, 2 - lag_index : 2 - lag_index + column_count]
        )
    return running


def modal_filter(values, residues, rates, skip_gain, initial):
    chan_count, seq_length = values.shape
    block_size = min(128, seq_length)
    block_count = seq_length // block_size
    set_width = min(chan_count, 32)
    set_count = chan_count // set_width

    def grouped(params):
        return jnp.moveaxis(params.reshape(params.shape[0], set_count, set_width), 1, 0)

    def state_combine(earlier, later):
        return (earlier[0] * later[0], earlier[1] * later[0] + later[1])

    def one_set(pieces_in):
        section, residue_set, rate_set, gain_set, initial_set = pieces_in
        lag_steps = jnp.arange(block_size, dtype=jnp.float32)
        rising = residue_set[:, :, None] * jnp.exp(-rate_set[:, :, None] * lag_steps)
        falling = jnp.exp(rate_set[:, :, None] * lag_steps)
        product = jnp.einsum("rci,rcj->cij", rising, falling, precision=HIGHEST)
        lower = (lag_steps[:, None] >= lag_steps[None, :])[None]
        matrix = jnp.where(lower, product, 0.0)
        blocks_in = section.reshape(set_width, block_count, block_size)
        within_block = split_product("cij,cbj->cbi", matrix, blocks_in)
        ending = jnp.exp(-rate_set[:, :, None] * (block_size - 1.0 - lag_steps))
        block_ends = split_product("rcj,cbj->cbr", ending, blocks_in)
        block_decay = jnp.broadcast_to(
            jnp.exp(-rate_set.T * block_size)[:, None, :], block_ends.shape
        )
        prefix_states = lax.associative_scan(state_combine, (block_decay, block_ends), axis=1)[1]
        entering = jnp.concatenate(
            [jnp.zeros_like(prefix_states[:, :1]), prefix_states[:, :-1]], axis=1
        )
        block_index = jnp.arange(block_count, dtype=jnp.float32)
        opening = jnp.exp(-rate_set[:, :, None] * block_size * block_index)
        entering = entering + jnp.einsum("rcb,rc->cbr", opening, initial_set, precision=HIGHEST)
        rise_decay = residue_set[:, :, None] * jnp.exp(-rate_set[:, :, None] * (lag_steps + 1.0))
        from_before = jnp.einsum("rci,cbr->cbi", rise_decay, entering, precision=HIGHEST)
        direct = gain_set[:, None, None] * blocks_in.astype(jnp.float32)
        return (within_block + from_before + direct).reshape(set_width, seq_length)

    outputs = lax.map(
        one_set,
        (
            values.reshape(set_count, set_width, seq_length),
            grouped(residues),
            grouped(rates),
            skip_gain.reshape(set_count, set_width),
            grouped(initial),
        ),
    )
    return outputs.reshape(chan_count, seq_length)


def local(
    stream_in,
    mr_proj,
    mr_short,
    mr_filter,
    mr_out,
    li_gain,
    li_in,
    li_short,
    li_res,
    li_rate,
    li_skip,
):
    row_count = mr_proj.shape[0]
    chan_width = mr_proj.shape[2]
    tap_count = mr_filter.shape[1]
    filter_count = mr_filter.shape[0]
    rim_rows = passed_along(mr_proj[-2:], "seq", 1)
    mr_mixed = lagged_rows(
        jnp.concatenate([rim_rows, mr_proj], axis=0).astype(jnp.float32), mr_short, row_count
    )
    queries = mr_mixed[:, 0]
    own_values = mr_mixed[:, 1] * mr_mixed[:, 2]
    tail_rows = passed_along(own_values[-(tap_count - 1) :].astype(jnp.bfloat16), "seq", 1).astype(
        jnp.float32
    )
    values_ext = jnp.concatenate([tail_rows, own_values], axis=0)
    block_count = row_count // tap_count
    padded = jnp.concatenate([values_ext, jnp.zeros((1, chan_width), jnp.float32)], axis=0)
    columns_major = padded.T.reshape(filter_count, GROUP, block_count + 1, tap_count)
    band_matrix = band_matrices(mr_filter)
    filtered_mr = jnp.einsum(
        "gis,gcbs->gcbi", band_matrix[:, :, :tap_count], columns_major[:, :, :-1], precision=HIGHEST
    )
    filtered_mr = filtered_mr + jnp.einsum(
        "gis,gcbs->gcbi", band_matrix[:, :, tap_count:], columns_major[:, :, 1:], precision=HIGHEST
    )
    filtered_rows = filtered_mr.reshape(chan_width, row_count).T
    gated = (queries * filtered_rows).astype(jnp.bfloat16)
    branch = jnp.dot(
        gated, lax.all_gather(mr_out, "seq", axis=1, tiled=True), preferred_element_type=jnp.float32
    )
    chan_start = lax.axis_index("chan") * chan_width
    summed = lax.psum(branch.astype(jnp.bfloat16), "chan").astype(jnp.float32)
    stream_full = (stream_in.astype(jnp.float32) + summed).astype(jnp.bfloat16)
    stream_out = lax.dynamic_slice_in_dim(stream_full, chan_start, chan_width, 1)
    stream_wide = stream_full.astype(jnp.float32)
    inverse_rms = lax.rsqrt(jnp.mean(stream_wide * stream_wide, axis=1, keepdims=True) + EPSILON)
    normed = (stream_wide * inverse_rms * li_gain[None]).astype(jnp.bfloat16)
    li_proj = jnp.einsum(
        "td,dpc->pct",
        normed,
        lax.all_gather(li_in, "seq", axis=0, tiled=True),
        preferred_element_type=jnp.float32,
    ).astype(jnp.bfloat16)
    li_rim_rows = passed_along(li_proj[:, :, -2:], "seq", 1)
    li_mixed = lagged_columns(
        jnp.concatenate([li_rim_rows, li_proj], axis=2).astype(jnp.float32), li_short, row_count
    )
    li_values = (li_mixed[1] * li_mixed[2]).astype(jnp.bfloat16)
    across = lax.all_to_all(li_values, "seq", split_axis=0, concat_axis=1, tiled=True)
    own_count = across.shape[0]
    seq_offset = lax.axis_index("seq") * own_count
    own_res = lax.dynamic_slice_in_dim(li_res, seq_offset, own_count, 1)
    own_rate = lax.dynamic_slice_in_dim(li_rate, seq_offset, own_count, 1)
    own_skip = lax.dynamic_slice_in_dim(li_skip, seq_offset, own_count, 0)
    zero_state = jnp.zeros((li_res.shape[0], own_count), jnp.float32)
    filtered_part = modal_filter(across, own_res, own_rate, own_skip, zero_state)
    li_filtered = lax.all_to_all(
        filtered_part.astype(jnp.bfloat16), "seq", split_axis=1, concat_axis=0, tiled=True
    ).astype(filtered_part.dtype)
    li_output = (li_mixed[0] * li_filtered).astype(jnp.bfloat16)
    return (stream_out, li_output)


def solution(mesh):
    in_specs = (
        P("seq", None),
        P("seq", None, "chan"),
        P(None, None, "chan"),
        P("chan", None),
        P("chan", "seq"),
        P(),
        P("seq", None, "chan"),
        P(None, None, "chan"),
        P(None, "chan"),
        P(None, "chan"),
        P("chan"),
    )
    out_specs = (P("seq", "chan"), P("chan", "seq"))
    return jax.shard_map(local, mesh=mesh, in_specs=in_specs, out_specs=out_specs, check_vma=False)
```

profile of v0, /device:TPU:9, one launch (start us, length us, event | category | flops | bytes accessed | tf_op | source)
XLA Modules:
  0.0 766.4 jit_solution(5964756891294948985)
XLA Ops:
  8.9 3.7 collective-permute-start
  13.8 6.1 fusion.50
  19.9 5.2 fusion.51
  25.1 8.9 %fusion.49 = f32[128,128,256]{0,2,1:T(8,128)} fusion(f32[128,128,256]{0,2,1:T(8,128)S(1)} %fusion.50, f32[128,128,256]{0,2,1:T(8,128)S(1)} %fusion.51, s32[128,256]{1,0:T(8,128)S(1)} %iota_subtract_fusion.1, f32[128,128]{1,0:T(8,128)S(1)} %copy-done.4), kind=kOutput, calls=%fused_computation.83 | convolution fusion | flops 1086341120 | bytes 50528256 | tf_op jit(solution)/shard_map/gj,isj->gis/dot_general | solution.py:29
  33.9 11.1 %slice_bitcast_fusion.1 = (f32[128,128,128,1]{0,2,1,3:T(8,128)}, f32[128,128,128,1]{0,2,1,3:T(8,128)}) fusion(f32[128,128,256]{0,2,1:T(8,128)} %fusion.49), kind=kLoop, calls=%fused_computation.89 | loop fusion | bytes 33554432 | tf_op jit(solution)/shard_map/slice | solution.py:149
  45.0 3.2 copy.177
  48.2 9.3 %copy.195 = f32[128,128,128,1]{2,1,3,0:T(8,128)} copy(f32[128,128,128,1]{0,2,1,3:T(8,128)} %get-tuple-element.100) | data formatting | bytes 16777216 | tf_op jit(solution)/shard_map/slice | solution.py:152
  57.6 9.4 %copy.194 = f32[128,128,128,1]{2,1,3,0:T(8,128)} copy(f32[128,128,128,1]{0,2,1,3:T(8,128)} %get-tuple-element.99) | data formatting | bytes 16777216 | tf_op jit(solution)/shard_map/slice | solution.py:149
  68.6 3.3 maximum_convert_fusion
  72.0 6.3 fusion.58
  78.7 2.2 collective-permute-start.1
  81.3 17.0 %collective-permute-done.1 = bf16[127,2048]{0,1:T(8,128)(2,1)S(1)} collective-permute-done((bf16[127,2048]{0,1:T(8,128)(2,1)S(1)}, bf16[127,2048]{0,1:T(8,128)(2,1)S(1)}, u32[]{:S(2)}, u32[]{:S(2)}) %collective-permute-start.1) | collective-permute-done | bytes 520224 | tf_op jit(solution)/shard_map/ppermute | solution.py:16
  99.2 3.0 reshape.133
  102.2 5.9 fusion.88
  108.1 15.8 %fusion.70 = f32[128,16,2,128]{3,1,2,0:T(8,128)S(1)} fusion(f32[128,128,128,1]{2,1,3,0:T(8,128)} %copy.195, f32[128,16,2,128]{3,2,1,0:T(2,128)S(1)} %get-tuple-element.102), kind=kOutput, calls=%fused_computation.126 | convolution fusion | flops 805306368 | bytes 12582912 | tf_op jit(solution)/shard_map/gis,gcbs->gcbi/dot_general | solution.py:151
  124.0 13.3 %fusion.76 = f32[128,16,2,128]{3,1,2,0:T(8,128)S(1)} fusion(f32[128,16,2,128]{3,1,2,0:T(8,128)S(1)} %fusion.70, f32[128,128,128,1]{2,1,3,0:T(8,128)S(1)} %bitcast.169, f32[128,16,2,128]{3,2,1,0:T(2,128)S(1)} %get-tuple-element.101), kind=kOutput, calls=%fused_computation.133 | convolution fusion | flops 805830656 | bytes 14680064 | tf_op jit(solution)/shard_map/gis,gcbs->gcbi/dot_general | solution.py:148
  139.8 12.8 %convolution_convert_fusion = bf16[256,4096]{1,0:T(8,128)(2,1)} fusion(bf16[2048,4096]{1,0:T(8,128)(2,1)} %all-gather.3.cloned.1.call-done, f32[256,8,2,128]{3,2,1,0:T(2,128)S(1)} %bitcast.170, f32[256,3,2048]{0,2,1:T(8,128)} %copy-done), kind=kOutput, calls=%fused_computation.105 | convolution fusion | flops 4297064448 | bytes 23068672 | tf_op jit(solution)/shard_map/dot_general | solution.py:156
  153.6 73.0 %all-reduce.13.cloned.1.call-done = bf16[256,4096]{1,0:T(8,128)(2,1)} async-done(((bf16[256,4096]{1,0:T(8,128)(2,1)}), bf16[256,4096]{1,0:T(8,128)(2,1)}) %all-reduce.13.cloned.1.call-update) | async-done | bytes 2097168 | tf_op jit(solution)/shard_map/psum | solution.py:160
  226.5 3.2 fusion.60
  229.7 246.0 %all-gather.5.cloned.1.call-done = bf16[4096,3,2048]{2,0,1:T(8,128)(2,1)} async-done(((bf16[256,3,2048]{2,0,1:T(8,128)(2,1)}), bf16[4096,3,2048]{2,0,1:T(8,128)(2,1)}) %all-gather.5.cloned.1.call-update) | async-done | bytes 50331664 | tf_op jit(solution)/shard_map/all_gather | solution.py:169
  475.8 20.5 %fusion.63 = bf16[3,2048,256]{1,2,0:T(8,128)(2,1)S(1)} fusion(bf16[4096,3,2048]{2,0,1:T(8,128)(2,1)} %all-gather.5.cloned.1.call-done, bf16[256,4096]{1,0:T(8,128)(2,1)S(1)} %get-tuple-element.86, f32[4096]{0:T(1024)S(1)} %copy-done.6, f32[256]{0:T(256)S(1)} %add_rsqrt_fusion), kind=kOutput, calls=%fused_computation.114 | convolution fusion | flops 12890669056 | bytes 55591936 | tf_op jit(solution)/shard_map/td,dpc->pct/dot_general | solution.py:166
  496.3 2.7 collective-permute-start.2
  502.8 2.6 copy-done.1
  507.2 7.4 all-to-all-start
  517.0 22.5 %all-to-all-done = bf16[16,128,256]{1,2,0:T(8,128)(2,1)S(1)} async-done(((bf16[16,128,256]{1,2,0:T(8,128)(2,1)}), bf16[16,128,256]{1,2,0:T(8,128)(2,1)S(1)}, u32[]{:S(2)}, u32[]{:S(2)}) %all-to-all-start) | async-done | bytes 1048608 | tf_op jit(solution)/shard_map/all_to_all | solution.py:177
  541.0 182.6 %while.10 = (s32[]{:T(128)}, bf16[4,32,4096]{2,1,0:T(8,128)(2,1)}, bf16[4,32,4096]{2,1,0:T(8,128)(2,1)S(1)}, f32[4,16,32]{1,2,0:T(8,128)}, f32[4,16,32]{2,0,1:T(...) while((s32[]{:T(128)}, bf16[4,32,4096]{2,1,0:T(8,128)(2,1)}, bf16[4,32,4096]{2,1,0:T(8,128)(2,1)S(1)}, ...), condition=%wide.region_3.4_spmd, body=%wide.region_2.3_spmd.sunk | while | flops 206249728 | bytes 13827589 | solution.py:104
  552.7 2.2 pad.98
  555.1 2.3 pad.97
  557.4 2.4 pad.100
  560.9 2.4 pad.99
  564.6 2.7 pad.102
  567.3 2.7 pad.101
  570.1 3.2 pad.104
  575.5 3.2 pad.103
  580.9 3.7 fusion.134
  598.3 2.2 pad.98
  600.7 2.3 pad.97
  603.0 2.4 pad.100
  606.5 2.4 pad.99
  610.2 2.7 pad.102
  612.9 2.7 pad.101
  615.7 3.2 pad.104
  621.0 3.2 pad.103
  626.5 3.7 fusion.134
  643.8 2.2 pad.98
  646.3 2.3 pad.97
  648.6 2.4 pad.100
  652.1 2.4 pad.99
  655.8 2.7 pad.102
  658.5 2.7 pad.101
  661.3 3.2 pad.104
  666.6 3.2 pad.103
  672.1 3.7 fusion.134
  689.4 2.2 pad.98
  691.9 2.3 pad.97
  694.2 2.4 pad.100
  697.7 2.4 pad.99
  701.4 2.7 pad.102
  704.1 2.7 pad.101
  706.9 3.2 pad.104
  712.2 3.2 pad.103
  717.7 3.7 fusion.134
  726.9 4.8 all-to-all-start.1
  732.7 23.9 %all-to-all-done.1 = bf16[128,16,256]{0,2,1:T(8,128)(2,1)S(1)} async-done(((bf16[128,16,256]{0,2,1:T(8,128)(2,1)}), bf16[128,16,256]{0,2,1:T(8,128)(2,1)S(1)}, u32[]{:S(2)}, u32[]{:S(2)}) %all-to-all-start.1) | async-done | bytes 1048608 | tf_op jit(solution)/shard_map/all_to_all | solution.py:185
  (284 shorter events, 108.7 us)
Async XLA Ops:
  7.2 132.6 %all-gather.3.cloned.1.call-start = ((), (), s32[]{:S(2)}) async-start(), calls=%async_computation.2 | async-start | bytes 17825792 | tf_op jit(solution)/shard_map/all_gather | solution.py:157
  7.9 218.6 %all-reduce.13.cloned.1.call-start = ((), (), s32[]{:S(2)}) async-start(), calls=%async_computation.3 | async-start | bytes 4194304 | tf_op jit(solution)/shard_map/psum | solution.py:160
  8.9 58.1 %collective-permute-start = (bf16[2,3,2048]{2,0,1:T(2,128)(2,1)S(1)}, bf16[2,3,2048]{2,0,1:T(2,128)(2,1)S(1)}, u32[]{:S(2)}, u32[]{:S(2)}) collective-permute-start(bf16[2,3,2048]{2,0,1:T(2,128)(2,1)S(1)} %slice.182), channel_id=1, source_target_pairs={{0,2},{2,4},{4,6},{6,8},{8,10},{10,12},{12,14},{14,16},{16,18},{18... | collective-permute-start | bytes 73736 | tf_op jit(solution)/shard_map/ppermute | solution.py:16
  13.8 6.1 copy-start.4
  78.2 3.0 copy-start
  78.7 19.5 %collective-permute-start.1 = (bf16[127,2048]{0,1:T(8,128)(2,1)S(1)}, bf16[127,2048]{0,1:T(8,128)(2,1)S(1)}, u32[]{:S(2)}, u32[]{:S(2)}) collective-permute-start(bf16[127,2048]{0,1:T(8,128)(2,1)S(1)} %fusion.81), channel_id=1, source_target_pairs={{0,2},{2,4},{4,6},{6,8},{8,10},{10,12},{12,14},{14,16},{16,18},{18... | collective-permute-start | bytes 1560584 | tf_op jit(solution)/shard_map/ppermute | solution.py:16
  102.2 21.8 %slice-start = ((s8[8388608]{0:T(1024)(128)(4,1)}), s8[4194304]{0:T(1024)(128)(4,1)S(1)}, s32[]{:S(2)}) async-start(s8[8388608]{0:T(1024)(128)(4,1)} %bitcast.168), calls=%async_computation.5 | async-start | bytes 8388608
  108.1 15.9 %slice-start.1 = ((s8[8388608]{0:T(1024)(128)(4,1)}), s8[4194304]{0:T(1024)(128)(4,1)S(1)}, s32[]{:S(2)}) async-start(s8[8388608]{0:T(1024)(128)(4,1)} %bitcast.168), calls=%async_computation.6 | async-start | bytes 8388608
  152.6 0.9 copy-start.5
  152.6 323.1 %copy-start.6 = (f32[4096]{0:T(1024)S(1)}, f32[4096]{0:T(1024)}, u32[]{:S(2)}) copy-start(f32[4096]{0:T(1024)} %param.18) | copy-start | bytes 49156
  152.7 323.1 %all-gather.5.cloned.1.call-start = ((), (), s32[]{:S(2)}) async-start(), calls=%async_computation.4 | async-start | bytes 53477376 | tf_op jit(solution)/shard_map/all_gather | solution.py:169
  229.7 266.5 %copy-start.2 = (bf16[256,4096]{1,0:T(8,128)(2,1)}, bf16[256,4096]{1,0:T(8,128)(2,1)S(1)}, u32[]{:S(2)}) copy-start(bf16[256,4096]{1,0:T(8,128)(2,1)S(1)} %get-tuple-element.86) | copy-start | bytes 6291460
  496.3 3.6 collective-permute-start.2
  502.8 2.6 copy-start.1
  507.2 32.3 %all-to-all-start = ((bf16[16,128,256]{1,2,0:T(8,128)(2,1)}), bf16[16,128,256]{1,2,0:T(8,128)(2,1)S(1)}, u32[]{:S(2)}, u32[]{:S(2)}) async-start(bf16[16,128,256]{1,2,0:T(8,128)(2,1)} %copy.185), calls=%async_computation | async-start | bytes 2097152 | tf_op jit(solution)/shard_map/all_to_all | solution.py:177
  723.6 8.1 %copy-start.3 = (bf16[256,4096]{1,0:T(8,128)(2,1)S(1)}, bf16[256,4096]{1,0:T(8,128)(2,1)}, u32[]{:S(2)}) copy-start(bf16[256,4096]{1,0:T(8,128)(2,1)} %copy-done.2) | copy-start | bytes 6291460
  726.9 29.7 %all-to-all-start.1 = ((bf16[128,16,256]{0,2,1:T(8,128)(2,1)}), bf16[128,16,256]{0,2,1:T(8,128)(2,1)S(1)}, u32[]{:S(2)}, u32[]{:S(2)}) async-start(bf16[128,16,256]{0,2,1:T(8,128)(2,1)} %copy.189), calls=%async_computation.1 | async-start | bytes 2097152 | tf_op jit(solution)/shard_map/all_to_all | solution.py:185
Sparse Core Ops, SparseCore 0:
  10.1 129.6 all-gather.2
  152.8 73.7 all-reduce.12
  228.1 247.6 all-gather.4
where the time goes:
time: 774 us; the launch traced here: 766 us
  waiting for transfers between devices  386 us (50%)
  local copies, waits for them, and re-layouts  205 us (26%)
  matrix products  110 us (14%)
  other arithmetic  28.4 us (4%)
  starting transfers between devices  20.9 us (3%)
  between operations  14.3 us (2%)
    all_gather x1, waiting for transfers between devices, local(): lax.all_gather(li_in, 'seq', axis=0, tiled=True)  246 us
    psum x1, waiting for transfers between devices, local(): summed = lax.psum(branch.astype(jnp.bfloat16), 'chan').astype(jnp.float32)  73 us
    pad x24, local copies, waits for them, and re-layouts, one_set(): lax.associative_scan(state_combine, (block_decay, block_ends), axis=1)[1]  58.9 us
    slice x52, local copies, waits for them, and re-layouts, one_set(): lax.associative_scan(state_combine, (block_decay, block_ends), axis=1)[1]  51.1 us
    all_to_all x1, waiting for transfers between devices, local(): lax.all_to_all(filtered_part.astype(jnp.bfloat16), 'seq', split_axis=1, c...  23.9 us
    all_to_all x1, waiting for transfers between devices, local(): lax.all_to_all(li_values, 'seq', split_axis=0, concat_axis=1, tiled=True)  22.5 us
    dot_general x1, matrix products, local(): jnp.einsum('td,dpc->pct', normed, lax.all_gather(li_in, 'seq', axis=0, ti...  20.5 us
    slice x2, local copies, waits for them, and re-layouts, local(): band_matrix[:, :, :tap_count]  20.4 us
  transfers between devices with their start and end apart: 8, of which 7 were waited for; matrix products, arithmetic and copies ran while one was open for 15% of the time, Pallas kernels for 0%

commit v1 on v0

v1 whole, which is shorter than its diff:
```python
import jax
import jax.numpy as jnp
from jax import lax
from jax.sharding import PartitionSpec as P

GROUP = 16


EPSILON = 1e-06
HIGHEST = lax.Precision.HIGHEST


def passed_along(block, axis, distance):
    devices = range(lax.axis_size(axis))
    route = [(i - distance, i) for i in devices if i - distance in devices]
    return lax.ppermute(block, axis, route)


def band_matrices(filters):
    tap_count = filters.shape[1]
    out_index = jnp.arange(tap_count, dtype=jnp.int32)[:, None, None]
    in_index = jnp.arange(2 * tap_count, dtype=jnp.int32)[None, :, None]
    lag_index = jnp.arange(tap_count, dtype=jnp.int32)[None, None, :]
    selector = (out_index + tap_count - 1 - in_index == lag_index).astype(jnp.bfloat16)
    return jnp.einsum(
        "gj,isj->gis", filters.astype(jnp.bfloat16), selector, preferred_element_type=jnp.float32
    ).astype(jnp.bfloat16)


def lagged_rows(extended, weights, row_count):
    running = weights[:, 0][None] * extended[2 : 2 + row_count]
    for lag_index in (1, 2):
        running = (
            running
            + weights[:, lag_index][None] * extended[2 - lag_index : 2 - lag_index + row_count]
        )
    return running


def swapped(blocks, axis):
    count = lax.axis_size(axis)
    if count != 2:
        return lax.all_to_all(blocks, axis, split_axis=0, concat_axis=0, tiled=True)
    me = lax.axis_index(axis)
    mine = lax.dynamic_index_in_dim(blocks, me, 0, keepdims=False)
    other = lax.dynamic_index_in_dim(blocks, 1 - me, 0, keepdims=False)
    received = lax.ppermute(other, axis, [(0, 1), (1, 0)])
    first = me == 0
    return jnp.stack([jnp.where(first, mine, received), jnp.where(first, received, mine)])


def summed_rows(blocks, axis):
    count = lax.axis_size(axis)
    if count != 2:
        return lax.psum_scatter(blocks.astype(jnp.bfloat16), axis, scatter_dimension=0).astype(
            jnp.float32
        )
    me = lax.axis_index(axis)
    mine = lax.dynamic_index_in_dim(blocks, me, 0, keepdims=False)
    other = lax.dynamic_index_in_dim(blocks, 1 - me, 0, keepdims=False).astype(jnp.bfloat16)
    return mine + lax.ppermute(other, axis, [(0, 1), (1, 0)]).astype(jnp.float32)


def modal_filter(values, residues, rates, skip_gain):
    chan_count, seq_length = values.shape
    size = min(128, seq_length)
    count = seq_length // size
    blocks_in = values.reshape(chan_count, count, size)
    lags = jnp.arange(size, dtype=jnp.float32)
    rising = residues[:, :, None] * jnp.exp(-rates[:, :, None] * lags)
    falling = jnp.exp(rates[:, :, None] * lags)
    product = jnp.einsum("rci,rcj->cij", rising, falling, precision=lax.Precision.HIGH)
    lower = (lags[:, None] >= lags[None, :])[None]
    matrix = jnp.where(lower, product, 0.0)
    matrix = matrix + jnp.where(
        lags[:, None] == lags[None, :], skip_gain[:, None, None], 0.0
    )
    within = jnp.einsum(
        "cij,cbj->cbi", matrix.astype(jnp.bfloat16), blocks_in, preferred_element_type=jnp.float32
    )
    ending = jnp.exp(-rates[:, :, None] * (size - 1.0 - lags)).astype(jnp.bfloat16)
    ends = jnp.einsum("rcj,cbj->rbc", ending, blocks_in, preferred_element_type=jnp.float32)
    index = jnp.arange(count, dtype=jnp.float32)
    apart = index[:, None] - 1.0 - index[None, :]
    decay = jnp.where(
        (apart >= 0.0)[None, :, :, None],
        jnp.exp(-rates[:, None, None, :] * size * jnp.maximum(apart, 0.0)[None, :, :, None]),
        0.0,
    )
    entering = jnp.sum(decay * ends[:, None], axis=2)
    rise_decay = residues[:, :, None] * jnp.exp(-rates[:, :, None] * (lags + 1.0))
    before = jnp.einsum(
        "rci,rbc->cbi",
        rise_decay.astype(jnp.bfloat16),
        entering.astype(jnp.bfloat16),
        preferred_element_type=jnp.float32,
    )
    return (within + before).reshape(chan_count, seq_length)


def lagged_time(rows, weights):
    length = rows.shape[1]
    padded = jnp.concatenate([jnp.zeros_like(rows[:, :2]), rows], axis=1).astype(jnp.float32)
    running = weights[0][:, None] * padded[:, 2:]
    for lag_index in (1, 2):
        running = running + weights[lag_index][:, None] * padded[:, 2 - lag_index : 2 - lag_index + length]
    return running


def local(
    stream_in,
    mr_proj,
    mr_short,
    mr_filter,
    mr_out,
    li_gain,
    li_in,
    li_short,
    li_res,
    li_rate,
    li_skip,
):
    row_count = mr_proj.shape[0]
    chan_width = mr_proj.shape[2]
    tap_count = mr_filter.shape[1]
    filter_count = mr_filter.shape[0]
    seq_size = lax.axis_size("seq")
    chan_size = lax.axis_size("chan")
    width = stream_in.shape[1]
    own_count = chan_width // seq_size
    part = row_count // chan_size
    me = lax.axis_index("chan")

    out_weights = lax.all_gather(mr_out.T, "seq", axis=0, tiled=True)

    in_blocks = li_in.reshape(li_in.shape[0], 3, seq_size, own_count)
    in_own = lax.all_to_all(
        jnp.transpose(in_blocks, (2, 1, 0, 3)), "seq", split_axis=0, concat_axis=0, tiled=True
    )
    in_own = jnp.transpose(in_own, (1, 0, 2, 3)).reshape(3, width, own_count)
    if chan_size == 2:
        in_other = lax.ppermute(in_own, "chan", [(0, 1), (1, 0)])
        first = me == 0
        in_all = jnp.stack(
            [jnp.where(first, in_own, in_other), jnp.where(first, in_other, in_own)]
        )
    else:
        in_all = lax.all_gather(in_own, "chan", axis=0)

    rim_rows = passed_along(mr_proj[-2:], "seq", 1)
    mr_mixed = lagged_rows(
        jnp.concatenate([rim_rows, mr_proj], axis=0).astype(jnp.float32), mr_short, row_count
    )
    queries = mr_mixed[:, 0]
    own_values = (mr_mixed[:, 1] * mr_mixed[:, 2]).astype(jnp.bfloat16)
    tail_rows = passed_along(own_values[-(tap_count - 1) :], "seq", 1)
    block_count = row_count // tap_count
    padded = jnp.concatenate(
        [tail_rows, own_values, jnp.zeros((1, chan_width), jnp.bfloat16)], axis=0
    )
    columns_major = padded.T.reshape(filter_count, GROUP, block_count + 1, tap_count)
    band_matrix = band_matrices(mr_filter)
    filtered_mr = jnp.einsum(
        "gis,gcbs->gcbi",
        band_matrix[:, :, :tap_count],
        columns_major[:, :, :-1],
        preferred_element_type=jnp.float32,
    )
    filtered_mr = filtered_mr + jnp.einsum(
        "gis,gcbs->gcbi",
        band_matrix[:, :, tap_count:],
        columns_major[:, :, 1:],
        preferred_element_type=jnp.float32,
    )
    filtered_rows = filtered_mr.reshape(chan_width, row_count).T
    gated = (queries * filtered_rows).astype(jnp.bfloat16)
    branch = jnp.einsum("tc,nc->tn", gated, out_weights, preferred_element_type=jnp.float32)
    summed = summed_rows(branch.reshape(chan_size, part, width), "chan")
    own_stream = lax.dynamic_slice_in_dim(stream_in, me * part, part, 0)
    stream = (own_stream.astype(jnp.float32) + summed).astype(jnp.bfloat16)
    stream_out = swapped(
        jnp.moveaxis(stream.reshape(part, chan_size, chan_width), 1, 0), "chan"
    ).reshape(row_count, chan_width)
    stream_wide = stream.astype(jnp.float32)
    inverse_rms = lax.rsqrt(jnp.mean(stream_wide * stream_wide, axis=1, keepdims=True) + EPSILON)
    normed = (stream_wide * inverse_rms * li_gain[None]).astype(jnp.bfloat16)
    gathered = lax.all_gather(normed, "seq", axis=0, tiled=True)

    def project(index):
        raw = jnp.einsum(
            "xdc,td->xct", in_all[:, index], gathered, preferred_element_type=jnp.float32
        ).astype(jnp.bfloat16)
        raw = swapped(raw, "chan").reshape(chan_size, own_count, seq_size, part)
        return jnp.transpose(raw, (1, 2, 0, 3)).reshape(own_count, seq_size * row_count)

    keys, gates, openers = project(1), project(2), project(0)
    seq_offset = lax.axis_index("seq") * own_count
    own_short = lax.dynamic_slice_in_dim(li_short, seq_offset, own_count, 2)
    own_res = lax.dynamic_slice_in_dim(li_res, seq_offset, own_count, 1)
    own_rate = lax.dynamic_slice_in_dim(li_rate, seq_offset, own_count, 1)
    own_skip = lax.dynamic_slice_in_dim(li_skip, seq_offset, own_count, 0)
    values = (lagged_time(keys, own_short[1]) * lagged_time(gates, own_short[2])).astype(
        jnp.bfloat16
    )
    filtered = modal_filter(values, own_res, own_rate, own_skip)
    result = (lagged_time(openers, own_short[0]) * filtered).astype(jnp.bfloat16)
    li_output = lax.all_to_all(result, "seq", split_axis=1, concat_axis=0, tiled=True)
    return (stream_out, li_output)


def solution(mesh):
    in_specs = (
        P("seq", None),
        P("seq", None, "chan"),
        P(None, None, "chan"),
        P("chan", None),
        P("chan", "seq"),
        P(),
        P("seq", None, "chan"),
        P(None, None, "chan"),
        P(None, "chan"),
        P(None, "chan"),
        P("chan"),
    )
    out_specs = (P("seq", "chan"), P("chan", "seq"))
    return jax.shard_map(local, mesh=mesh, in_specs=in_specs, out_specs=out_specs, check_vma=False)
```

time: 774 us -> 515 us (0.67)
  waiting for transfers between devices: 386 us -> 168 us
  local copies, waits for them, and re-layouts: 205 us -> 58.7 us
  blocking collectives: 0 us -> 136 us
  matrix products: 110 us -> 77.5 us
    all_gather x2, waiting for transfers between devices: 247 us -> 64.1 us  [the longest x1 64.1 us: local(): out_weights = lax.all_gather(mr_out.T, 'seq', axis=0, tiled=True)]
    all_to_all x0 -> x1, blocking collectives: none -> 136 us  [local(): lax.all_to_all(jnp.transpose(in_blocks, (2, 1, 0, 3)), 'seq', split_axis=...]
    ppermute x0 -> x6, waiting for transfers between devices: none -> 90.7 us  [the longest x1 54.6 us: local(): in_other = lax.ppermute(in_own, 'chan', [(0, 1), (1, 0)])]
    psum x1 -> x0, waiting for transfers between devices: 73 us -> none  [local(): summed = lax.psum(branch.astype(jnp.bfloat16), 'chan').astype(jnp.float32)]
    slice x59 -> x2, local copies, waits for them, and re-layouts: 69.8 us -> 1.71 us  [the longest x1 1.5 us: local(): columns_major[:, :, 1:]]
    pad x24 -> x0, local copies, waits for them, and re-layouts: 58.9 us -> none  [one_set(): lax.associative_scan(state_combine, (block_decay, block_ends), axis=1)[1]]
    all_to_all x2 -> x1, waiting for transfers between devices: 46.4 us -> 7.09 us  [local(): lax.all_to_all(result, 'seq', split_axis=1, concat_axis=0, tiled=True)]
    slice x2 -> x1, local copies, waits for them, and re-layouts: 20.4 us -> 6.73 us  [local(): band_matrix[:, :, :tap_count]]
  transfers between devices with their start and end apart: 8 -> 11, of which waited for: 7 -> 6; matrix products, arithmetic and copies ran while one was open for 15% -> 26% of each run, Pallas kernels for 0% -> 0%
where the time goes in v1:
time: 515 us; the launch traced here: 509 us
  waiting for transfers between devices  168 us (33%)
  blocking collectives  136 us (26%)
  matrix products  77.5 us (15%)
  local copies, waits for them, and re-layouts  58.7 us (11%)
  other arithmetic  35 us (7%)
  starting transfers between devices  18.9 us (4%)
  between operations  14.8 us (3%)
    all_to_all x1, blocking collectives, local(): lax.all_to_all(jnp.transpose(in_blocks, (2, 1, 0, 3)), 'seq', split_axis=...  136 us
    all_gather x1, waiting for transfers between devices, local(): out_weights = lax.all_gather(mr_out.T, 'seq', axis=0, tiled=True)  64.1 us
    ppermute x1, waiting for transfers between devices, local(): in_other = lax.ppermute(in_own, 'chan', [(0, 1), (1, 0)])  54.6 us
    dot_general x3, matrix products, project(): jnp.einsum('xdc,td->xct', in_all[:, index], gathered, preferred_element_t...  35.5 us
    ppermute x1, waiting for transfers between devices, summed_rows(): lax.ppermute(other, axis, [(0, 1), (1, 0)]).astype(jnp.float32)  23.3 us
    ppermute x4, waiting for transfers between devices, swapped(): received = lax.ppermute(other, axis, [(0, 1), (1, 0)])  12.9 us
    unnamed x29, local copies, waits for them, and re-layouts  12.6 us
    slice x2, local copies, waits for them, and re-layouts, local(): band_matrix[:, :, tap_count:]  10.6 us
  transfers between devices with their start and end apart: 11, of which 6 were waited for; matrix products, arithmetic and copies ran while one was open for 26% of the time, Pallas kernels for 0%

profile of v1, /device:TPU:9, one launch (start us, length us, event | category | flops | bytes accessed | tf_op | source)
XLA Modules:
  0.0 508.8 jit_solution(13683285514748106525)
XLA Ops:
  7.9 0.9 slice.133
  8.9 3.7 collective-permute-start
  12.7 8.5 %convert_bitcast_fusion = bf16[128,128,256]{0,2,1:T(8,128)(2,1)S(1)} fusion(s32[128,256]{1,0:T(8,128)S(1)} %iota_subtract_fusion, f32[128,128]{1,0:T(8,128)} %param.14), kind=kOutput, calls=%fused_computation.10 | convolution fusion | flops 1082146816 | bytes 8585216 | tf_op jit(solution)/shard_map/gj,isj->gis/dot_general | solution.py:25
  21.3 3.9 slice_bitcast_fusion
  25.2 3.2 copy.127
  28.4 6.7 %copy.157 = bf16[128,128,128,1]{2,1,3,0:T(8,128)(2,1)} copy(bf16[128,128,128,1]{0,2,1,3:T(8,128)(2,1)} %get-tuple-element.7) | data formatting | bytes 8388608 | tf_op jit(solution)/shard_map/slice | solution.py:165
  35.1 6.7 %copy.158 = bf16[128,128,128,1]{2,1,3,0:T(8,128)(2,1)} copy(bf16[128,128,128,1]{0,2,1,3:T(8,128)(2,1)} %get-tuple-element.6) | data formatting | bytes 8388608 | tf_op jit(solution)/shard_map/slice | solution.py:171
  41.9 1.6 copy.126
  43.4 3.3 maximum_convert_fusion
  46.8 6.3 %fusion.8 = f32[256,3,2048]{0,2,1:T(8,128)S(1)} fusion(f32[258,3,2048]{0,2,1:T(8,128)S(1)} %maximum_convert_fusion, f32[3,2048]{1,0:T(4,128)S(1)} %get-tuple-element.34, f32[3,2048]{1,0:T(4,128)S(1)} %get-tuple-element.35, f32[3,2048]{1,0:T(4,128)S(1)} %bitcast.187), kind=kLoop, calls=%fused_computation.17 | loop fusion | flops 7864320 | bytes 25239552 | tf_op jit(solution)/shard_map/add | solution.py:34
  53.5 2.1 collective-permute-start.1
  55.9 5.6 %collective-permute-done.1 = bf16[127,2048]{0,1:T(8,128)(2,1)S(1)} collective-permute-done((bf16[127,2048]{0,1:T(8,128)(2,1)S(1)}, bf16[127,2048]{0,1:T(8,128)(2,1)S(1)}, u32[]{:S(2)}, u32[]{:S(2)}) %collective-permute-start.1) | collective-permute-done | bytes 520224 | tf_op jit(solution)/shard_map/ppermute | solution.py:16
  61.5 2.1 maximum_bitcast_fusion
  63.6 4.0 reshape.213
  67.6 1.5 fusion.87
  69.1 0.8 copy-done.1
  70.0 2.3 fusion.55
  72.2 2.3 convolution_add_fusion.1
  74.5 1.1 copy.132
  75.6 64.1 %all-gather.3.cloned.1.call-done = bf16[4096,2048]{0,1:T(8,128)(2,1)} async-done(((bf16[256,2048]{0,1:T(8,128)(2,1)}), bf16[4096,2048]{0,1:T(8,128)(2,1)}) %all-gather.3.cloned.1.call-update) | async-done | bytes 16777232 | tf_op jit(solution)/shard_map/all_gather | solution.py:134
  139.8 8.7 %fusion.52 = f32[256,4096]{1,0:T(8,128)S(1)} fusion(bf16[4096,2048]{0,1:T(8,128)(2,1)} %all-gather.3.cloned.1.call-done, f32[256,8,2,128]{3,2,1,0:T(2,128)S(1)} %bitcast.171, f32[256,3,2048]{0,2,1:T(8,128)} %copy-done), kind=kOutput, calls=%fused_computation.83 | convolution fusion | flops 4296015872 | bytes 25165824 | tf_op jit(solution)/shard_map/tc,nc->tn/dot_general | solution.py:177
  148.5 2.0 copy-done.3
  150.6 1.2 collective-permute-start.2
  151.9 23.3 %collective-permute-done.2 = bf16[128,4096]{1,0:T(8,128)(2,1)S(1)} collective-permute-done((bf16[128,4096]{1,0:T(8,128)(2,1)S(1)}, bf16[128,4096]{1,0:T(8,128)(2,1)S(1)}, u32[]{:S(2)}, u32[]{:S(2)}) %collective-permute-start.2) | collective-permute-done | bytes 1048608 | tf_op jit(solution)/shard_map/ppermute | solution.py:61
  175.1 2.4 fusion.24
  177.6 1.0 copy-done.4
  178.5 1.3 fusion.26
  179.8 3.2 copy.135
  183.2 135.6 %all_to_all.24 = bf16[16,3,256,128]{2,3,1,0:T(8,128)(2,1)S(1)} all-to-all(bf16[16,3,256,128]{2,3,1,0:T(8,128)(2,1)S(1)} %copy.136), channel_id=1, replica_groups=mesh['seq'=16,'chan'=2] {'seq'}, dimensions={0} | all-to-all | bytes 6291456 | tf_op jit(solution)/shard_map/all_to_all | solution.py:137
  319.3 1.3 collective-permute-start.4
  321.6 0.8 dynamic_slice.55
  322.4 0.9 fusion.79
  323.5 9.8 %fusion.57 = f32[128,128,128]{2,1,0:T(8,128)} fusion(f32[16,128]{0,1:T(8,128)S(1)} %copy.150, f32[16,128]{0,1:T(8,128)S(1)} %copy.149, f32[16,128]{0,1:T(8,128)S(1)} %copy.148), kind=kOutput, calls=%fused_computation.93 | convolution fusion | flops 202113024 | bytes 8413184 | tf_op jit(solution)/shard_map/rci,rcj->cij/dot_general | solution.py:72
  333.2 54.6 %collective-permute-done.4 = bf16[3,4096,128]{1,2,0:T(8,128)(2,1)} collective-permute-done((bf16[3,4096,128]{1,2,0:T(8,128)(2,1)S(1)}, bf16[3,4096,128]{1,2,0:T(8,128)(2,1)}, u32[]{:S(2)}, u32[]{:S(2)}) %collective-permute-start.4) | collective-permute-done | bytes 3145760 | tf_op jit(solution)/shard_map/ppermute | solution.py:142
  387.8 4.9 select_bitcast_fusion
  392.8 12.1 %fusion.18 = bf16[2,128,2048]{2,1,0:T(8,128)(2,1)} fusion(bf16[2048,4096]{1,0:T(8,128)(2,1)} %all-gather.5.cloned.1.call-done, bf16[1,3,4096,128]{2,3,0,1:T(8,128)(2,1)} %get-tuple-element.9, bf16[1,3,4096,128]{2,3,0,1:T(8,128)(2,1)} %get-tuple-element.8), kind=kOutput, calls=%fused_computation.34 | convolution fusion | flops 4296540160 | bytes 24117248 | tf_op jit(solution)/shard_map/xdc,td->xct/dot_general | solution.py:190
  404.8 1.9 dynamic-slice_bitcast_fusion.1
  406.7 1.2 collective-permute-start.6
  407.9 11.6 %fusion.21 = bf16[2,128,2048]{2,1,0:T(8,128)(2,1)} fusion(bf16[2048,4096]{1,0:T(8,128)(2,1)} %all-gather.5.cloned.1.call-done, bf16[1,3,4096,128]{2,3,0,1:T(8,128)(2,1)S(1)} %copy-done.7, bf16[1,3,4096,128]{2,3,0,1:T(8,128)(2,1)} %get-tuple-element.9), kind=kOutput, calls=%fused_computation.35 | convolution fusion | flops 4296540160 | bytes 24117248 | tf_op jit(solution)/shard_map/xdc,td->xct/dot_general | solution.py:190
  419.6 1.9 dynamic-slice_bitcast_fusion
  421.7 11.8 %fusion.15 = bf16[2,128,2048]{2,1,0:T(8,128)(2,1)} fusion(bf16[2048,4096]{1,0:T(8,128)(2,1)} %all-gather.5.cloned.1.call-done, bf16[1,3,4096,128]{2,3,0,1:T(8,128)(2,1)} %get-tuple-element.9, bf16[1,3,4096,128]{2,3,0,1:T(8,128)(2,1)S(1)} %copy-done.7), kind=kOutput, calls=%fused_computation.33 | convolution fusion | flops 4296540160 | bytes 24117248 | tf_op jit(solution)/shard_map/xdc,td->xct/dot_general | solution.py:190
  433.5 1.9 dynamic-slice_bitcast_fusion.2
  435.4 1.2 collective-permute-start.5
  436.6 1.3 bitcast_select_fusion.3
  438.9 0.9 copy-done.9
  439.8 1.1 bitcast_select_fusion.1
  440.9 1.0 copy.145
  442.3 1.1 maximum_bitcast_fusion.3
  443.7 1.4 fusion.37
  445.1 1.0 copy.151
  447.2 7.1 %fusion.10 = f32[128,32,128]{2,1,0:T(8,128)} fusion(bf16[128,32,128]{2,1,0:T(8,128)(2,1)S(1)} %copy.151, f32[128,128,128]{2,1,0:T(8,128)} %fusion.57, f32[128]{0:T(128)S(1)} %dynamic_slice.55, pred[128,128]{1,0:T(8,128)(4,1)S(1)} %get-tuple-element.37, pred[128,128]{1,0:T(8,128)(4,1)S(1)} %get-tuple-element.38), kind=kOutput, calls=%fused_computation.22 | convolution fusion | flops 142606336 | bytes 11567616 | tf_op jit(solution)/shard_map/cij,cbj->cbi/dot_general | solution.py:78
  454.3 3.4 multiply_reduce_fusion
  458.1 2.7 convolution_add_fusion
  460.8 2.1 copy.163
  462.9 1.1 bitcast_select_fusion.5
  465.0 1.3 copy-done.6
  466.3 1.7 fusion.46
  468.0 7.5 %all-to-all-start.1 = ((bf16[128,16,256]{0,2,1:T(8,128)(2,1)}), bf16[128,16,256]{0,2,1:T(8,128)(2,1)S(1)}, u32[]{:S(2)}, u32[]{:S(2)}) async-start(bf16[128,16,256]{0,2,1:T(8,128)(2,1)} %bitcast.58), calls=%async_computation.1 | async-start | bytes 2097152 | tf_op jit(solution)/shard_map/all_to_all | solution.py:207
  475.5 0.8 reshape.216
  476.3 2.2 constant_dynamic-slice_fusion.7
  479.1 12.8 %collective-permute-done.3 = bf16[128,2048]{1,0:T(8,128)(2,1)S(1)} collective-permute-done((bf16[128,2048]{1,0:T(8,128)(2,1)S(1)}, bf16[128,2048]{1,0:T(8,128)(2,1)S(1)}, u32[]{:S(2)}, u32[]{:S(2)}) %collective-permute-start.3) | collective-permute-done | bytes 524320 | tf_op jit(solution)/shard_map/ppermute | solution.py:47
  492.3 1.1 pad_maximum_fusion.1
  493.4 7.1 %all-to-all-done.1 = bf16[128,16,256]{0,2,1:T(8,128)(2,1)S(1)} async-done(((bf16[128,16,256]{0,2,1:T(8,128)(2,1)}), bf16[128,16,256]{0,2,1:T(8,128)(2,1)S(1)}, u32[]{:S(2)}, u32[]{:S(2)}) %all-to-all-start.1) | async-done | bytes 1048608 | tf_op jit(solution)/shard_map/all_to_all | solution.py:207
  500.4 1.3 copy.156
  (72 shorter events, 9.0 us)
Async XLA Ops:
  7.2 132.6 %all-gather.3.cloned.1.call-start = ((), (), s32[]{:S(2)}) async-start(), calls=%async_computation.2 | async-start | bytes 17825792 | tf_op jit(solution)/shard_map/all_gather | solution.py:134
  7.9 384.9 %all-gather.5.cloned.1.call-start = ((), (), s32[]{:S(2)}) async-start(), calls=%async_computation.3 | async-start | bytes 17825792 | tf_op jit(solution)/shard_map/all_gather | solution.py:187
  8.9 33.0 %collective-permute-start = (bf16[2,3,2048]{2,0,1:T(2,128)(2,1)S(1)}, bf16[2,3,2048]{2,0,1:T(2,128)(2,1)S(1)}, u32[]{:S(2)}, u32[]{:S(2)}) collective-permute-start(bf16[2,3,2048]{2,0,1:T(2,128)(2,1)S(1)} %slice.133), channel_id=1, source_target_pairs={{0,2},{2,4},{4,6},{6,8},{8,10},{10,12},{12,14},{14,16},{16,18},{18... | collective-permute-start | bytes 73736 | tf_op jit(solution)/shard_map/ppermute | solution.py:16
  12.7 8.5 %copy-start.10 = (f32[3,3,2048]{2,1,0:T(4,128)S(1)}, f32[3,3,2048]{2,1,0:T(4,128)}, u32[]{:S(2)}) copy-start(f32[3,3,2048]{2,1,0:T(4,128)} %param.13) | copy-start | bytes 221188
  53.0 2.6 copy-start
  53.5 8.0 %collective-permute-start.1 = (bf16[127,2048]{0,1:T(8,128)(2,1)S(1)}, bf16[127,2048]{0,1:T(8,128)(2,1)S(1)}, u32[]{:S(2)}, u32[]{:S(2)}) collective-permute-start(bf16[127,2048]{0,1:T(8,128)(2,1)S(1)} %slice_bitcast_fusion.3), channel_id=1, source_target_pairs={{0,2},{2,4},{4,6},{6,8},{8,10},{10,12},{12,14},{14,16},{16,18},{18... | collective-permute-start | bytes 1560584 | tf_op jit(solution)/shard_map/ppermute | solution.py:16
  67.6 2.3 copy-start.1
  69.9 2.3 copy-start.2
  148.5 2.0 copy-start.3
  150.6 27.9 %copy-start.11 = (f32[4096]{0:T(1024)S(1)}, f32[4096]{0:T(1024)}, u32[]{:S(2)}) copy-start(f32[4096]{0:T(1024)} %param.16) | copy-start | bytes 49156
  150.6 24.5 %collective-permute-start.2 = (bf16[128,4096]{1,0:T(8,128)(2,1)S(1)}, bf16[128,4096]{1,0:T(8,128)(2,1)S(1)}, u32[]{:S(2)}, u32[]{:S(2)}) collective-permute-start(bf16[128,4096]{1,0:T(8,128)(2,1)S(1)} %fusion.51), channel_id=1, source_target_pairs={{0,1},{1,0},{2,3},{3,2},{4,5},{5,4},{6,7},{7,6},{8,9},{9,8},{10,11... | collective-permute-start | bytes 3145736 | tf_op jit(solution)/shard_map/ppermute | solution.py:61
  177.5 1.0 copy-start.4
  319.3 68.6 %collective-permute-start.4 = (bf16[3,4096,128]{1,2,0:T(8,128)(2,1)S(1)}, bf16[3,4096,128]{1,2,0:T(8,128)(2,1)}, u32[]{:S(2)}, u32[]{:S(2)}) collective-permute-start(bf16[3,4096,128]{1,2,0:T(8,128)(2,1)S(1)} %bitcast.169), channel_id=1, source_target_pairs={{0,1},{1,0},{2,3},{3,2},{4,5},{5,4},{6,7},{7,6},{8,9},{9,8},{10,11... | collective-permute-start | bytes 9437192 | tf_op jit(solution)/shard_map/ppermute | solution.py:142
  392.8 15.2 %copy-start.7 = (bf16[1,3,4096,128]{2,3,0,1:T(8,128)(2,1)S(1)}, bf16[1,3,4096,128]{2,3,0,1:T(8,128)(2,1)}, u32[]{:S(2)}) copy-start(bf16[1,3,4096,128]{2,3,0,1:T(8,128)(2,1)} %get-tuple-element.8) | copy-start | bytes 9437188
  406.7 29.9 %collective-permute-start.6 = (bf16[128,2048]{1,0:T(8,128)(2,1)}, bf16[128,2048]{1,0:T(8,128)(2,1)}, u32[]{:S(2)}, u32[]{:S(2)}) collective-permute-start(bf16[128,2048]{1,0:T(8,128)(2,1)} %dynamic-slice_bitcast_fusion.1), channel_id=1, source_target_pairs={{0,1},{1,0},{2,3},{3,2},{4,5},{5,4},{6,7},{7,6},{8,9},{9,8},{10,11... | collective-permute-start | bytes 1572872 | tf_op jit(solution)/shard_map/ppermute | solution.py:47
  421.5 17.4 %collective-permute-start.7 = (bf16[128,2048]{1,0:T(8,128)(2,1)}, bf16[128,2048]{1,0:T(8,128)(2,1)}, u32[]{:S(2)}, u32[]{:S(2)}) collective-permute-start(bf16[128,2048]{1,0:T(8,128)(2,1)} %dynamic-slice_bitcast_fusion), channel_id=1, source_target_pairs={{0,1},{1,0},{2,3},{3,2},{4,5},{5,4},{6,7},{7,6},{8,9},{9,8},{10,11... | collective-permute-start | bytes 1572872 | tf_op jit(solution)/shard_map/ppermute | solution.py:47
  435.4 27.5 %collective-permute-start.5 = (bf16[128,2048]{1,0:T(8,128)(2,1)}, bf16[128,2048]{1,0:T(8,128)(2,1)}, u32[]{:S(2)}, u32[]{:S(2)}) collective-permute-start(bf16[128,2048]{1,0:T(8,128)(2,1)} %dynamic-slice_bitcast_fusion.2), channel_id=1, source_target_pairs={{0,1},{1,0},{2,3},{3,2},{4,5},{5,4},{6,7},{7,6},{8,9},{9,8},{10,11... | collective-permute-start | bytes 1572872 | tf_op jit(solution)/shard_map/ppermute | solution.py:47
  438.6 1.2 copy-start.9
  460.8 2.1 copy-start.8
  464.7 1.6 copy-start.6
  466.3 9.2 %copy-start.5 = (bf16[128,4096]{1,0:T(8,128)(2,1)S(1)}, bf16[128,4096]{1,0:T(8,128)(2,1)}, u32[]{:S(2)}) copy-start(bf16[128,4096]{1,0:T(8,128)(2,1)} %copy-done.4) | copy-start | bytes 3145732
  468.0 32.4 %all-to-all-start.1 = ((bf16[128,16,256]{0,2,1:T(8,128)(2,1)}), bf16[128,16,256]{0,2,1:T(8,128)(2,1)S(1)}, u32[]{:S(2)}, u32[]{:S(2)}) async-start(bf16[128,16,256]{0,2,1:T(8,128)(2,1)} %bitcast.58), calls=%async_computation.1 | async-start | bytes 2097152 | tf_op jit(solution)/shard_map/all_to_all | solution.py:207
  478.8 13.2 %collective-permute-start.3 = (bf16[128,2048]{1,0:T(8,128)(2,1)S(1)}, bf16[128,2048]{1,0:T(8,128)(2,1)S(1)}, u32[]{:S(2)}, u32[]{:S(2)}) collective-permute-start(bf16[128,2048]{1,0:T(8,128)(2,1)S(1)} %bitcast.186), channel_id=1, source_target_pairs={{0,1},{1,0},{2,3},{3,2},{4,5},{5,4},{6,7},{7,6},{8,9},{9,8},{10,11... | collective-permute-start | bytes 1572872 | tf_op jit(solution)/shard_map/ppermute | solution.py:47
Sparse Core Ops, SparseCore 0:
  10.1 129.5 all-gather.2
  180.0 178.8 all-gather.4
